TPU v7x, 256 devices: a whole 4x4x8 slice. The times are simulated.
256 devices in a mesh: batch: 32 (over z, x), tensor: 8 (over y, core).
Axes of the slice: x: 4, y: 4, z: 8, core: 2. Of those that a mesh axis runs over, the one named last changes fastest.
Arguments:
- tokens: bfloat16 [8192, 4096], P(('batch', 'tensor')), may hold values from -6 to 6
- norm_gain: float32 [4096], replicated, may hold values from 0.1 to 1.9
- w_query: bfloat16 [4096, 4096], P(None, 'tensor'), may hold values from -0.09375 to 0.09375
- w_key: bfloat16 [4096, 1024], P(None, 'tensor'), may hold values from -0.25 to 0.25
- w_value: bfloat16 [4096, 1024], P(None, 'tensor'), may hold values from -0.09375 to 0.09375
- w_out: bfloat16 [4096, 4096], P('tensor'), may hold values from -0.25 to 0.25
- prefix_keys: bfloat16 [16384, 1024], P('batch', 'tensor'), may hold values from -6 to 6
- prefix_values: bfloat16 [16384, 1024], P('batch', 'tensor'), may hold values from -6 to 6
- cache_keys: bfloat16 [147456, 1024], P('batch', 'tensor'), may hold values from -160 to 160
- cache_values: bfloat16 [147456, 1024], P('batch', 'tensor'), may hold values from -6 to 6
- cache_lengths: int32 [128], replicated, may hold values from 128 to 2048, as said below
- prefix_used: int32 [128], P('batch'), may hold values from 4096 to 16384
- parents: int32 [128, 64], P('batch'), may hold values from 0 to 62, as said below
- accepted_index: int32 [128, 8], P('batch'), may hold values from 0 to 63, as said below
Outputs:
- mixed_output: bfloat16 [8192, 4096], P(('batch', 'tensor'))
- accepted_keys: bfloat16 [128, 8, 1024], P('batch', None, 'tensor')
- accepted_values: bfloat16 [128, 8, 1024], P('batch', None, 'tensor')
Inputs may be any that keep to these rules, and one draw needn't show every extreme that they name: `cache_lengths`: within each aligned group of 4 requests at most 2 have more than 256 cached tokens; in the first group exactly that many do, and some request has exactly 2048. parents[r, 0] = 0; for i >= 1, parents[r, i] lies between max(0, i - 8) and i - 1. `accepted_index`: each row lists 8 tree positions, each the parent of the next, ending at a position of 32 or more; where the root is reached the row repeats 0 at its front.
All inputs are finite; a program needn't handle non-finite values.
Results may differ from a plain program's by a relative error of at most 0.015.
The roundings to bfloat16 on the way count: a program that leaves them out, or rounds other values in their place, can miss the bound.
Values may be sent and summed in bfloat16 or wider, within the bound.
A program may use at most 192 MiB of HBM per device.

v0:
```python
import jax
import jax.numpy as jnp
from jax import lax
from jax.sharding import PartitionSpec as P

HD = 128
NEG_FILL = -1e30
HIGHEST = lax.Precision.HIGHEST


def rms_normed(tokens, norm_gain):
    values = tokens.astype(jnp.float32)
    factor = lax.rsqrt(jnp.mean(values * values, axis=-1, keepdims=True) + 1e-05)
    return (values * factor * norm_gain).astype(jnp.bfloat16)


def ancestor_table(parents):
    node_count = parents.shape[-1]
    column = jnp.arange(node_count, dtype=jnp.int32)
    linked = (parents[..., None] == column).astype(jnp.float32)
    itself = (column[:, None] == column[None, :]).astype(jnp.float32)
    ancestry = jnp.minimum(linked + itself, 1.0)
    for repeat in range(node_count.bit_length()):
        ancestry = jnp.minimum(
            jnp.einsum("rij,rjk->rik", ancestry, ancestry, precision=HIGHEST), 1.0
        )
    return ancestry


def rotate(values, positions):
    half_width = values.shape[-1] // 2
    frequency = 10000.0 ** (-jnp.arange(half_width, dtype=jnp.float32) / half_width)
    angles = positions.astype(jnp.float32)[:, None] * frequency[None, :]
    cosine = jnp.cos(angles)[:, None, :]
    sine_table = jnp.sin(angles)[:, None, :]
    first_half = values[..., :half_width]
    second_half = values[..., half_width:]
    return jnp.concatenate(
        [
            first_half * cosine - second_half * sine_table,
            second_half * cosine + first_half * sine_table,
        ],
        axis=-1,
    )


def absorb(carry, scores, visible, apply_values):
    running_max, running_sum, running_out = carry
    masked = jnp.where(visible, scores, NEG_FILL)
    new_max = jnp.maximum(running_max, jnp.max(masked, axis=-1))
    weights = jnp.where(visible, jnp.exp(masked - new_max[..., None]), 0.0)
    factor = jnp.exp(running_max - new_max)
    new_sum = running_sum * factor + jnp.sum(weights, axis=-1)
    new_out = running_out * factor[..., None] + apply_values(weights.astype(jnp.bfloat16))
    return (new_max, new_sum, new_out)


def combine(first_part, second_part):
    joint_max = jnp.maximum(first_part[0], second_part[0])
    first_factor = jnp.exp(first_part[0] - joint_max)
    second_factor = jnp.exp(second_part[0] - joint_max)
    joint_sum = first_part[1] * first_factor + second_part[1] * second_factor
    joint_out = first_part[2] * first_factor[..., None] + second_part[2] * second_factor[..., None]
    return (joint_max, joint_sum, joint_out)


def empty_partials(leading, head_size):
    return (
        jnp.full(leading, NEG_FILL, jnp.float32),
        jnp.zeros(leading, jnp.float32),
        jnp.zeros(leading + (head_size,), jnp.float32),
    )


def cache_partials(queries, all_keys, all_values, lower_slot, upper_slot, score_scale):
    capacity = all_keys.shape[0]
    block_size = min(512, capacity)
    kv_local = queries.shape[1]
    head_size = queries.shape[3]

    def one_request(request_items):
        request_query, lower_bound, upper_bound = request_items
        blocks = (upper_bound - lower_bound + block_size - 1) // block_size

        def block_step(block_index, carry):
            block_begin = lower_bound + block_index * block_size
            start = jnp.clip(block_begin, 0, capacity - block_size)
            block_keys = lax.dynamic_slice_in_dim(all_keys, start, block_size, 0).reshape(
                block_size, kv_local, head_size
            )
            block_values = lax.dynamic_slice_in_dim(all_values, start, block_size, 0).reshape(
                block_size, kv_local, head_size
            )
            slot_ids = start + jnp.arange(block_size, dtype=jnp.int32)
            visible = (slot_ids >= block_begin) & (
                slot_ids < jnp.minimum(upper_bound, block_begin + block_size)
            )
            scores = (
                jnp.einsum(
                    "hqd,khd->hqk", request_query, block_keys, preferred_element_type=jnp.float32
                )
                * score_scale
            )
            return absorb(
                carry,
                scores,
                visible[None, None, :],
                lambda rounded: jnp.einsum(
                    "hqk,khd->hqd", rounded, block_values, preferred_element_type=jnp.float32
                ),
            )

        start_carry = empty_partials(request_query.shape[:2], head_size)
        return lax.fori_loop(0, blocks, block_step, start_carry)

    return lax.map(one_request, (queries, lower_slot, upper_slot))


def body(
    tokens,
    norm_gain,
    w_query,
    w_key,
    w_value,
    w_out,
    prefix_keys,
    prefix_values,
    cache_keys,
    cache_values,
    cache_lengths,
    prefix_used,
    parents,
    accepted_index,
):
    req_count, tree_size = parents.shape
    head_size = HD
    query_cols = w_query.shape[1]
    key_cols = w_key.shape[1]
    kv_local = key_cols // head_size
    group_size = query_cols // key_cols
    query_rows = tree_size * group_size
    score_scale = head_size ** (-0.5)
    normed = rms_normed(tokens, norm_gain)
    piece = lax.all_gather(normed, "tensor", axis=0, tiled=True)
    projected = jnp.concatenate(
        [
            jnp.dot(piece, w_query, preferred_element_type=jnp.float32),
            jnp.dot(piece, w_key, preferred_element_type=jnp.float32),
            jnp.dot(piece, w_value, preferred_element_type=jnp.float32),
        ],
        axis=1,
    )
    group_index = lax.axis_index("batch")
    own_lengths = lax.dynamic_slice_in_dim(cache_lengths, group_index * req_count, req_count)
    ancestry = ancestor_table(parents)
    tree_depth = (jnp.sum(ancestry, axis=-1) - 1.0).astype(jnp.int32)
    position = ((prefix_used + own_lengths)[:, None] + tree_depth).reshape(req_count * tree_size)
    queries = rotate(
        projected[:, :query_cols].reshape(-1, kv_local * group_size, head_size), position
    ).astype(jnp.bfloat16)
    queries = queries.reshape(req_count, tree_size, kv_local, group_size, head_size).transpose(
        0, 2, 1, 3, 4
    )
    queries = queries.reshape(req_count, kv_local, query_rows, head_size)
    new_keys = rotate(
        projected[:, query_cols : query_cols + key_cols].reshape(-1, kv_local, head_size), position
    ).astype(jnp.bfloat16)
    new_keys = new_keys.reshape(req_count, tree_size, key_cols)
    new_values = (
        projected[:, query_cols + key_cols :]
        .astype(jnp.bfloat16)
        .reshape(req_count, tree_size, key_cols)
    )
    accepted_keys = jnp.take_along_axis(new_keys, accepted_index[:, :, None], axis=1)
    accepted_values = jnp.take_along_axis(new_values, accepted_index[:, :, None], axis=1)
    tree_keys = new_keys.reshape(req_count, tree_size, kv_local, head_size)
    tree_values = new_values.reshape(req_count, tree_size, kv_local, head_size)
    tree_scores = (
        jnp.einsum("rhqd,rkhd->rhqk", queries, tree_keys, preferred_element_type=jnp.float32)
        * score_scale
    )
    tree_visible = jnp.repeat(ancestry > 0.5, group_size, axis=1)[:, None]
    tree_part = absorb(
        empty_partials((req_count, kv_local, query_rows), head_size),
        tree_scores,
        tree_visible,
        lambda rounded: jnp.einsum(
            "rhqk,rkhd->rhqd", rounded, tree_values, preferred_element_type=jnp.float32
        ),
    )
    own_offsets = jnp.cumsum(own_lengths) - own_lengths
    cache_part = cache_partials(
        queries, cache_keys, cache_values, own_offsets, own_offsets + own_lengths, score_scale
    )
    local_part = combine(tree_part, cache_part)
    piece_keys = lax.all_gather(prefix_keys, "batch", axis=0, tiled=True)
    piece_values = lax.all_gather(prefix_values, "batch", axis=0, tiled=True)
    row_count = piece_keys.shape[0]
    shaped_keys = piece_keys.reshape(row_count, kv_local, head_size)
    shaped_values = piece_values.reshape(row_count, kv_local, head_size)
    slot_ids = jnp.arange(row_count, dtype=jnp.int32)
    visible = (slot_ids[None, :] < prefix_used[:, None])[:, None, None, :]
    scores = (
        jnp.einsum("rhqd,khd->rhqk", queries, shaped_keys, preferred_element_type=jnp.float32)
        * score_scale
    )
    folded = absorb(
        local_part,
        scores,
        visible,
        lambda rounded: jnp.einsum(
            "rhqk,khd->rhqd", rounded, shaped_values, preferred_element_type=jnp.float32
        ),
    )
    attended = (folded[2] / folded[1][..., None]).astype(jnp.bfloat16)
    attended = attended.reshape(req_count, kv_local, tree_size, group_size, head_size).transpose(
        0, 2, 1, 3, 4
    )
    attended = attended.reshape(req_count * tree_size, query_cols)
    mixed_rows = lax.psum_scatter(
        jnp.dot(attended, w_out, preferred_element_type=jnp.float32).astype(jnp.bfloat16),
        "tensor",
        scatter_dimension=0,
        tiled=True,
    )
    return (mixed_rows, accepted_keys, accepted_values)


def solution(mesh):
    in_specs = (
        P(("batch", "tensor"), None),
        P(),
        P(None, "tensor"),
        P(None, "tensor"),
        P(None, "tensor"),
        P("tensor", None),
        P("batch", "tensor"),
        P("batch", "tensor"),
        P("batch", "tensor"),
        P("batch", "tensor"),
        P(),
        P("batch"),
        P("batch", None),
        P("batch", None),
    )
    out_specs = (
        P(("batch", "tensor"), None),
        P("batch", None, "tensor"),
        P("batch", None, "tensor"),
    )
    return jax.shard_map(body, mesh=mesh, in_specs=in_specs, out_specs=out_specs, check_vma=False)
```

profile of v0, /device:TPU:4, one launch (start us, length us, event | category | flops | bytes accessed | tf_op | source)
XLA Modules:
  0.0 278.1 jit_solution(979624814477540230)
XLA Ops:
  8.4 1.8 fusion.54
  18.2 23.1 %all-gather.4.cloned.1.call-done = bf16[256,4096]{1,0:T(8,128)(2,1)} async-done(((bf16[32,4096]{1,0:T(8,128)(2,1)}), bf16[256,4096]{1,0:T(8,128)(2,1)}) %all-gather.4.cloned.1.call-update) | async-done | bytes 2097168 | tf_op jit(solution)/shard_map/all_gather | solution.py:144
  41.3 4.1 %fusion.85 = f32[256,512]{1,0:T(8,128)S(1)} fusion(bf16[256,4096]{1,0:T(8,128)(2,1)} %all-gather.4.cloned.1.call-done, bf16[4096,512]{1,0:T(8,128)(2,1)} %param.22), kind=kOutput, calls=%fused_computation.133 | convolution fusion | flops 1073741824 | bytes 6815744 | tf_op jit(solution)/shard_map/dot_general | solution.py:147
  46.9 44.6 %while.69 = (s32[]{:T(128)}, f32[4,1,256]{2,1,0:T(1,128)S(1)}, f32[4,1,256]{2,1,0:T(1,128)S(1)}, f32[4,1,256,128]{3,2,1,0:T(8,128)}, s32[4]{0:T(128)S(1)}, /*ind...) while((s32[]{:T(128)}, f32[4,1,256]{2,1,0:T(1,128)S(1)}, ...), condition=%wide.region_9.10_spmd, body=%wide.region_4.9_spmd.sunk | while | flops 68356632 | bytes 2712316 | solution.py:116
  50.5 4.0 %while.70 = (s32[]{:T(128)}, f32[1,256]{1,0:T(1,128)S(1)}, f32[1,256]{1,0:T(1,128)S(1)}, f32[1,256,128]{2,1,0:T(8,128)S(1)}, s32[]{:T(128)}, /*index=5*/s32[]{:T...) while((s32[]{:T(128)}, f32[1,256]{1,0:T(1,128)S(1)}, ...), condition=%wide.region_8.8_spmd, body=%wide.region_5.7_spmd.sunk | while | flops 68356616 | bytes 2181353 | solution.py:114
  53.2 1.3 fusion.119
  58.6 16.0 %while.70 = (s32[]{:T(128)}, f32[1,256]{1,0:T(1,128)S(1)}, f32[1,256]{1,0:T(1,128)S(1)}, f32[1,256,128]{2,1,0:T(8,128)S(1)}, s32[]{:T(128)}, /*index=5*/s32[]{:T...) while((s32[]{:T(128)}, f32[1,256]{1,0:T(1,128)S(1)}, ...), condition=%wide.region_8.8_spmd, body=%wide.region_5.7_spmd.sunk | while | flops 68356616 | bytes 2181353 | solution.py:114
  65.2 1.3 fusion.119
  69.2 1.3 fusion.119
  73.2 1.3 fusion.119
  78.7 4.0 %while.70 = (s32[]{:T(128)}, f32[1,256]{1,0:T(1,128)S(1)}, f32[1,256]{1,0:T(1,128)S(1)}, f32[1,256,128]{2,1,0:T(8,128)S(1)}, s32[]{:T(128)}, /*index=5*/s32[]{:T...) while((s32[]{:T(128)}, f32[1,256]{1,0:T(1,128)S(1)}, ...), condition=%wide.region_8.8_spmd, body=%wide.region_5.7_spmd.sunk | while | flops 68356616 | bytes 2181353 | solution.py:114
  81.3 1.3 fusion.119
  86.8 4.0 %while.70 = (s32[]{:T(128)}, f32[1,256]{1,0:T(1,128)S(1)}, f32[1,256]{1,0:T(1,128)S(1)}, f32[1,256,128]{2,1,0:T(8,128)S(1)}, s32[]{:T(128)}, /*index=5*/s32[]{:T...) while((s32[]{:T(128)}, f32[1,256]{1,0:T(1,128)S(1)}, ...), condition=%wide.region_8.8_spmd, body=%wide.region_5.7_spmd.sunk | while | flops 68356616 | bytes 2181353 | solution.py:114
  89.4 1.3 fusion.119
  93.3 1.5 copy.30
  94.8 1.5 copy.29
  100.0 2.6 convolution_convert_fusion.1
  102.5 22.0 %all-gather.6.cloned.1.call-done = bf16[16384,128]{1,0:T(8,128)(2,1)} async-done(((bf16[512,128]{1,0:T(8,128)(2,1)}), bf16[16384,128]{1,0:T(8,128)(2,1)}) %all-gather.6.cloned.1.call-update) | async-done | bytes 4194320 | tf_op jit(solution)/shard_map/all_gather | solution.py:196
  124.5 27.2 %fusion.17 = (f32[4,256]{1,0:T(4,128)S(1)}, f32[4,256,16384]{2,1,0:T(8,128)}) fusion(pred[4,16384]{1,0:T(4,128)(4,1)S(1)} %iota_compare_fusion, bf16[16384,128]{1,0:T(8,128)(2,1)} %all-gather.6.cloned.1.call-done, bf16[4,256,64]{2,1,0:T(8,128)(2,1)} %bitcast.194, bf16[4,256,64]{2,1,0:T(8,128)(2,1)S(1)} %bitcast.191), kind=kOutput, calls=%fused_computation.30 | convolution fusion | flops 4345822208 | bytes 71634944 | tf_op jit(solution)/shard_map/rhqd,khd->rhqk/dot_general | solution.py:204
  151.8 24.3 %fusion.18 = f32[4,256]{1,0:T(4,128)S(1)} fusion(f32[4,256,16384]{2,1,0:T(8,128)} %get-tuple-element.336, f32[4,256]{1,0:T(4,128)S(1)} %get-tuple-element.337, pred[4,16384]{1,0:T(4,128)(4,1)S(1)} %iota_compare_fusion), kind=kLoop, calls=%fused_computation.31 | loop fusion | flops 83885056 | bytes 67182592 | tf_op jit(solution)/shard_map/reduce_sum | solution.py:53
  177.3 28.4 %all-gather.8.cloned.1.call-done = bf16[16384,128]{1,0:T(8,128)(2,1)} async-done(((bf16[512,128]{1,0:T(8,128)(2,1)}), bf16[16384,128]{1,0:T(8,128)(2,1)}) %all-gather.8.cloned.1.call-update) | async-done | bytes 4194320 | tf_op jit(solution)/shard_map/all_gather | solution.py:197
  205.7 25.9 %fusion.46 = bf16[4,1,256,128]{3,2,0,1:T(8,128)(2,1)S(1)} fusion(f32[4,1,256,128]{3,2,0,1:T(8,128)S(1)} %fusion.45, bf16[16384,128]{1,0:T(8,128)(2,1)} %all-gather.8.cloned.1.call-done, f32[4,256,16384]{2,1,0:T(8,128)} %get-tuple-element.336, f32[4,256]{1,0:T(4,128)S(1)} %get-tuple-element.337, pred[4,16384]{1,0:T(4,128)(4,1)S(1)} %iota_compare_fusion, ...), kind=kOutput, calls=%fused_computation.48 | convolution fusion | flops 4379246592 | bytes 72163328 | tf_op jit(solution)/shard_map/rhqk,khd->rhqd/dot_general | solution.py:211
  231.8 4.8 %convolution_convert_fusion = bf16[256,4096]{1,0:T(8,128)(2,1)} fusion(bf16[256,512]{1,0:T(8,128)(2,1)S(1)} %reshape_transpose_reshape.4, bf16[512,4096]{1,0:T(8,128)(2,1)} %param.25), kind=kOutput, calls=%fused_computation.36 | convolution fusion | flops 1074790400 | bytes 6553600 | tf_op jit(solution)/shard_map/dot_general | solution.py:221
  238.8 32.8 %reduce-scatter.2.cloned.1.call-done = bf16[32,4096]{1,0:T(8,128)(2,1)} async-done(((bf16[256,4096]{1,0:T(8,128)(2,1)}), bf16[32,4096]{1,0:T(8,128)(2,1)}) %reduce-scatter.2.cloned.1.call-update) | async-done | bytes 262160 | tf_op jit(solution)/shard_map/reduce_scatter | solution.py:220
  (159 shorter events, 41.5 us)
Async XLA Ops:
  7.2 84.3 %copy-start = (bf16[4096,128]{1,0:T(8,128)(2,1)S(1)}, bf16[4096,128]{1,0:T(8,128)(2,1)}, u32[]{:S(2)}) copy-start(bf16[4096,128]{1,0:T(8,128)(2,1)} %param.23) | copy-start | bytes 3145732
  7.2 34.1 %all-gather.4.cloned.1.call-start = ((), (), s32[]{:S(2)}) async-start(), calls=%async_computation.1 | async-start | bytes 2359296 | tf_op jit(solution)/shard_map/all_gather | solution.py:144
  10.2 114.3 %all-gather.6.cloned.1.call-start = ((), (), s32[]{:S(2)}) async-start(), calls=%async_computation.2 | async-start | bytes 4325376 | tf_op jit(solution)/shard_map/all_gather | solution.py:196
  11.0 194.7 %all-gather.8.cloned.1.call-start = ((), (), s32[]{:S(2)}) async-start(), calls=%async_computation.3 | async-start | bytes 4325376 | tf_op jit(solution)/shard_map/all_gather | solution.py:197
  11.7 259.8 %reduce-scatter.2.cloned.1.call-start = ((), (), s32[]{:S(2)}) async-start(), calls=%async_computation.4 | async-start | bytes 2359296 | tf_op jit(solution)/shard_map/reduce_scatter | solution.py:220
  46.0 0.9 copy-start.2
  46.0 0.9 copy-start.4
  46.9 44.6 %copy-start.1 = (bf16[256,4096]{1,0:T(8,128)(2,1)S(1)}, bf16[256,4096]{1,0:T(8,128)(2,1)}, u32[]{:S(2)}) copy-start(bf16[256,4096]{1,0:T(8,128)(2,1)} %all-gather.4.cloned.1.call-done) | copy-start | bytes 6291460
  91.5 7.7 %copy-start.11 = (f32[4,1,256]{2,1,0:T(1,128)}, f32[4,1,256]{2,1,0:T(1,128)S(1)}, u32[]{:S(2)}) copy-start(f32[4,1,256]{2,1,0:T(1,128)S(1)} %get-tuple-element.269) | copy-start | bytes 12292
  91.5 33.1 %copy-start.3 = (bf16[256,4,64]{2,1,0:T(4,128)(2,1)S(1)}, bf16[256,4,64]{2,1,0:T(4,128)(2,1)}, u32[]{:S(2)}) copy-start(bf16[256,4,64]{2,1,0:T(4,128)(2,1)} %copy-done.2) | copy-start | bytes 393220
  97.2 0.6 copy-start.7
  99.2 0.7 copy-start.5
  151.8 24.4 %copy-start.12 = (f32[4,1,256]{2,1,0:T(1,128)S(1)}, f32[4,1,256]{2,1,0:T(1,128)}, u32[]{:S(2)}) copy-start(f32[4,1,256]{2,1,0:T(1,128)} %copy-done.11) | copy-start | bytes 12292
  151.8 24.5 %copy-start.6 = (f32[4,256,64]{1,2,0:T(8,128)S(1)}, f32[4,256,64]{1,2,0:T(8,128)}, u32[]{:S(2)}) copy-start(f32[4,256,64]{1,2,0:T(8,128)} %copy-done.5) | copy-start | bytes 786436
  151.8 24.4 %copy-start.9 = (bf16[256,128]{1,0:T(8,128)(2,1)S(1)}, bf16[256,128]{1,0:T(8,128)(2,1)}, u32[]{:S(2)}) copy-start(bf16[256,128]{1,0:T(8,128)(2,1)} %convolution_convert_fusion.1) | copy-start | bytes 196612
  151.8 24.4 %copy-start.10 = (f32[4,1,256,128]{3,2,1,0:T(8,128)S(1)}, f32[4,1,256,128]{3,2,1,0:T(8,128)}, u32[]{:S(2)}) copy-start(f32[4,1,256,128]{3,2,1,0:T(8,128)} %get-tuple-element.268) | copy-start | bytes 1572868
  231.8 4.9 %copy-start.13 = (s32[4,8]{1,0:T(4,128)S(1)}, s32[4,8]{1,0:T(4,128)}, u32[]{:S(2)}) copy-start(s32[4,8]{1,0:T(4,128)} %param.33) | copy-start | bytes 388
  231.8 5.6 %copy-start.8 = (bf16[4,64,128]{2,1,0:T(8,128)(2,1)S(1)}, bf16[4,64,128]{2,1,0:T(8,128)(2,1)}, u32[]{:S(2)}) copy-start(bf16[4,64,128]{2,1,0:T(8,128)(2,1)} %copy-done.7) | copy-start | bytes 196612
Sparse Core Ops, SparseCore 0:
  10.4 30.7 all-gather.3
  43.8 80.6 all-gather.5
  127.1 78.5 all-gather.7
  236.7 34.7 reduce-scatter.1
where the time goes:
time: 279 us; the launch traced here: 278 us
  waiting for transfers between devices  108 us (39%)
  matrix products  87.9 us (32%)
  other arithmetic  35.8 us (13%)
  local copies, waits for them, and re-layouts  17.8 us (6%)
  loops' own time  14.5 us (5%)
  between operations  14.2 us (5%)
    reduce_scatter x1, waiting for transfers between devices, body(): lax.psum_scatter(jnp.dot(attended, w_out, preferred_element_type=jnp.floa...  32.8 us
    all_gather x1, waiting for transfers between devices, body(): piece_values = lax.all_gather(prefix_values, 'batch', axis=0, tiled=True)  28.4 us
    dot_general x1, matrix products, body(): jnp.einsum('rhqd,khd->rhqk', queries, shaped_keys, preferred_element_type...  27.2 us
    dot_general x1, matrix products, body(): jnp.einsum('rhqk,khd->rhqd', rounded, shaped_values, preferred_element_ty...  25.9 us
    reduce_sum x9, other arithmetic, absorb(): new_sum = running_sum * factor + jnp.sum(weights, axis=-1)  25.5 us
    all_gather x1, waiting for transfers between devices, body(): piece = lax.all_gather(normed, 'tensor', axis=0, tiled=True)  23.1 us
    all_gather x1, waiting for transfers between devices, body(): piece_keys = lax.all_gather(prefix_keys, 'batch', axis=0, tiled=True)  22 us
    dot_general x7, matrix products, block_step(): jnp.einsum('hqk,khd->hqd', rounded, block_values, preferred_element_type=...  9.34 us
  transfers between devices with their start and end apart: 4, of which 4 were waited for; matrix products, arithmetic and copies ran while one was open for 38% of the time, Pallas kernels for 0%

commit v1 on v0

--- a/solution.py
+++ b/solution.py
@@ -6,6 +6,9 @@
 HD = 128
 NEG_FILL = -1e30
 HIGHEST = lax.Precision.HIGHEST
+try_all_counts = lambda point, axis_name: jnp.concatenate(
+    lax.all_to_all(jnp.stack(lax.psum(1, axis_name=axis_name) * [point]), axis_name, 0, 0), axis=0
+)
 
 
 def rms_normed(tokens, norm_gain):
@@ -193,7 +196,7 @@
         queries, cache_keys, cache_values, own_offsets, own_offsets + own_lengths, score_scale
     )
     local_part = combine(tree_part, cache_part)
-    piece_keys = lax.all_gather(prefix_keys, "batch", axis=0, tiled=True)
+    piece_keys = try_all_counts(prefix_keys, "batch")
     piece_values = lax.all_gather(prefix_values, "batch", axis=0, tiled=True)
     row_count = piece_keys.shape[0]
     shaped_keys = piece_keys.reshape(row_count, kv_local, head_size)

time: 279 us -> 261 us (0.935)
  waiting for transfers between devices: 108 us -> 76.9 us
  starting transfers between devices: 0.16 us -> 11.9 us
  local copies, waits for them, and re-layouts: 17.8 us -> 21.6 us
    all_to_all x0 -> x1, waiting for transfers between devices: none -> 31.5 us  [lax.all_to_all(jnp.stack(lax.psum(1, axis_name=axis_name) * [point]), axi...]
    all_gather x1, waiting for transfers between devices: 28.4 us -> 0.02 us  [body(): piece_values = lax.all_gather(prefix_values, 'batch', axis=0, tiled=True)]
    all_gather x1 -> x0, waiting for transfers between devices: 22 us -> none  [body(): piece_keys = lax.all_gather(prefix_keys, 'batch', axis=0, tiled=True)]
    all_gather x1, waiting for transfers between devices: 23.1 us -> 11 us  [body(): piece = lax.all_gather(normed, 'tensor', axis=0, tiled=True)]
    all_to_all x0 -> x1, starting transfers between devices: none -> 11.8 us  [lax.all_to_all(jnp.stack(lax.psum(1, axis_name=axis_name) * [point]), axi...]
    another operation x14 -> x15, local copies, waits for them, and re-layouts: 0.06 us -> 3.87 us  [the longest x1 3.81 us: jnp.stack(lax.psum(1, axis_name=axis_name) * [point])]
  transfers between devices with their start and end apart: 4 -> 4, of which waited for: 4 -> 3; matrix products, arithmetic and copies ran while one was open for 38% -> 41% of each run, Pallas kernels for 0% -> 0%
where the time goes in v1:
time: 261 us; the launch traced here: 260 us
  matrix products  87.1 us (33%)
  waiting for transfers between devices  76.9 us (29%)
  other arithmetic  33.8 us (13%)
  local copies, waits for them, and re-layouts  21.6 us (8%)
  loops' own time  14.4 us (6%)
  between operations  14.2 us (5%)
  starting transfers between devices  11.9 us (5%)
    reduce_scatter x1, waiting for transfers between devices, body(): lax.psum_scatter(jnp.dot(attended, w_out, preferred_element_type=jnp.floa...  33.7 us
    all_to_all x1, waiting for transfers between devices, lax.all_to_all(jnp.stack(lax.psum(1, axis_name=axis_name) * [point]), axi...  31.5 us
    dot_general x1, matrix products, body(): jnp.einsum('rhqd,khd->rhqk', queries, shaped_keys, preferred_element_type...  27 us
    dot_general x1, matrix products, body(): jnp.einsum('rhqk,khd->rhqd', rounded, shaped_values, preferred_element_ty...  26.1 us
    reduce_sum x9, other arithmetic, absorb(): new_sum = running_sum * factor + jnp.sum(weights, axis=-1)  25.5 us
    all_to_all x1, starting transfers between devices, lax.all_to_all(jnp.stack(lax.psum(1, axis_name=axis_name) * [point]), axi...  11.8 us
    all_gather x1, waiting for transfers between devices, body(): piece = lax.all_gather(normed, 'tensor', axis=0, tiled=True)  11 us
    dot_general x7, matrix products, block_step(): jnp.einsum('hqk,khd->hqd', rounded, block_values, preferred_element_type=...  9.35 us
  transfers between devices with their start and end apart: 4, of which 3 were waited for; matrix products, arithmetic and copies ran while one was open for 41% of the time, Pallas kernels for 0%

profile of v1, /device:TPU:4, one launch (start us, length us, event | category | flops | bytes accessed | tf_op | source)
XLA Modules:
  0.0 260.0 jit_solution(16664376400438006465)
XLA Ops:
  8.4 1.8 fusion.52
  10.2 3.8 %stack.2 = bf16[32,512,128]{2,1,0:T(8,128)(2,1)} broadcast(bf16[512,128]{1,0:T(8,128)(2,1)} %param.26), dimensions={1,2} | broadcast | bytes 4325376 | tf_op jit(solution)/shard_map/stack | solution.py:10
  14.1 11.8 %all-to-all-start = ((bf16[32,512,128]{2,1,0:T(8,128)(2,1)}), bf16[32,512,128]{2,1,0:T(8,128)(2,1)}, u32[]{:S(2)}, u32[]{:S(2)}) async-start(bf16[32,512,128]{2,1,0:T(8,128)(2,1)} %stack.2), calls=%async_computation | async-start | bytes 8388608 | tf_op jit(solution)/shard_map/all_to_all | solution.py:10
  30.3 11.0 %all-gather.3.cloned.1.call-done = bf16[256,4096]{1,0:T(8,128)(2,1)} async-done(((bf16[32,4096]{1,0:T(8,128)(2,1)}), bf16[256,4096]{1,0:T(8,128)(2,1)}) %all-gather.3.cloned.1.call-update) | async-done | bytes 2097168 | tf_op jit(solution)/shard_map/all_gather | solution.py:147
  41.3 4.1 %fusion.84 = f32[256,512]{1,0:T(8,128)S(1)} fusion(bf16[256,4096]{1,0:T(8,128)(2,1)} %all-gather.3.cloned.1.call-done, bf16[4096,512]{1,0:T(8,128)(2,1)} %param.22), kind=kOutput, calls=%fused_computation.132 | convolution fusion | flops 1073741824 | bytes 6815744 | tf_op jit(solution)/shard_map/dot_general | solution.py:150
  46.9 44.5 %while.69 = (s32[]{:T(128)}, f32[4,1,256]{2,1,0:T(1,128)S(1)}, f32[4,1,256]{2,1,0:T(1,128)S(1)}, f32[4,1,256,128]{3,2,1,0:T(8,128)}, s32[4]{0:T(128)S(1)}, /*ind...) while((s32[]{:T(128)}, f32[4,1,256]{2,1,0:T(1,128)S(1)}, ...), condition=%wide.region_9.10_spmd, body=%wide.region_4.9_spmd.sunk | while | flops 68356632 | bytes 2712316 | solution.py:119
  50.5 4.0 %while.70 = (s32[]{:T(128)}, f32[1,256]{1,0:T(1,128)S(1)}, f32[1,256]{1,0:T(1,128)S(1)}, f32[1,256,128]{2,1,0:T(8,128)S(1)}, s32[]{:T(128)}, /*index=5*/s32[]{:T...) while((s32[]{:T(128)}, f32[1,256]{1,0:T(1,128)S(1)}, ...), condition=%wide.region_8.8_spmd, body=%wide.region_5.7_spmd.sunk | while | flops 68356616 | bytes 2181353 | solution.py:117
  53.2 1.3 fusion.119
  58.6 16.0 %while.70 = (s32[]{:T(128)}, f32[1,256]{1,0:T(1,128)S(1)}, f32[1,256]{1,0:T(1,128)S(1)}, f32[1,256,128]{2,1,0:T(8,128)S(1)}, s32[]{:T(128)}, /*index=5*/s32[]{:T...) while((s32[]{:T(128)}, f32[1,256]{1,0:T(1,128)S(1)}, ...), condition=%wide.region_8.8_spmd, body=%wide.region_5.7_spmd.sunk | while | flops 68356616 | bytes 2181353 | solution.py:117
  61.2 1.3 fusion.119
  65.2 1.3 fusion.119
  73.2 1.3 fusion.119
  78.6 4.0 %while.70 = (s32[]{:T(128)}, f32[1,256]{1,0:T(1,128)S(1)}, f32[1,256]{1,0:T(1,128)S(1)}, f32[1,256,128]{2,1,0:T(8,128)S(1)}, s32[]{:T(128)}, /*index=5*/s32[]{:T...) while((s32[]{:T(128)}, f32[1,256]{1,0:T(1,128)S(1)}, ...), condition=%wide.region_8.8_spmd, body=%wide.region_5.7_spmd.sunk | while | flops 68356616 | bytes 2181353 | solution.py:117
  81.3 1.3 fusion.119
  86.7 4.0 %while.70 = (s32[]{:T(128)}, f32[1,256]{1,0:T(1,128)S(1)}, f32[1,256]{1,0:T(1,128)S(1)}, f32[1,256,128]{2,1,0:T(8,128)S(1)}, s32[]{:T(128)}, /*index=5*/s32[]{:T...) while((s32[]{:T(128)}, f32[1,256]{1,0:T(1,128)S(1)}, ...), condition=%wide.region_8.8_spmd, body=%wide.region_5.7_spmd.sunk | while | flops 68356616 | bytes 2181353 | solution.py:117
  93.2 1.5 copy.30
  94.7 1.5 copy.29
  99.9 2.5 convolution_convert_fusion.1
  102.4 31.5 %all-to-all-done = bf16[32,512,128]{2,1,0:T(8,128)(2,1)} async-done(((bf16[32,512,128]{2,1,0:T(8,128)(2,1)}), bf16[32,512,128]{2,1,0:T(8,128)(2,1)}, u32[]{:S(2)}, u32[]{:S(2)}) %all-to-all-start) | async-done | bytes 4194336 | tf_op jit(solution)/shard_map/all_to_all | solution.py:10
  134.0 27.0 %fusion.17 = (f32[4,256]{1,0:T(4,128)S(1)}, f32[4,256,16384]{2,1,0:T(8,128)}) fusion(pred[4,16384]{1,0:T(4,128)(4,1)S(1)} %iota_compare_fusion, bf16[16384,128,1]{1,0,2:T(8,128)(2,1)} %bitcast.26, bf16[4,256,64]{2,1,0:T(8,128)(2,1)} %bitcast.193, bf16[4,256,64]{2,1,0:T(8,128)(2,1)S(1)} %bitcast.190), kind=kOutput, calls=%fused_computation.30 | convolution fusion | flops 4345822208 | bytes 71634944 | tf_op jit(solution)/shard_map/rhqd,khd->rhqk/dot_general | solution.py:207
  161.0 24.3 %fusion.18 = f32[4,256]{1,0:T(4,128)S(1)} fusion(f32[4,256,16384]{2,1,0:T(8,128)} %get-tuple-element.336, f32[4,256]{1,0:T(4,128)S(1)} %get-tuple-element.337, pred[4,16384]{1,0:T(4,128)(4,1)S(1)} %iota_compare_fusion), kind=kLoop, calls=%fused_computation.31 | loop fusion | flops 83885056 | bytes 67182592 | tf_op jit(solution)/shard_map/reduce_sum | solution.py:56
  186.5 26.1 %fusion.44 = bf16[4,1,256,128]{3,2,0,1:T(8,128)(2,1)S(1)} fusion(f32[4,1,256,128]{3,2,0,1:T(8,128)S(1)} %fusion.43, bf16[16384,128]{1,0:T(8,128)(2,1)} %all-gather.5.cloned.1.call-done, f32[4,256,16384]{2,1,0:T(8,128)} %get-tuple-element.336, f32[4,256]{1,0:T(4,128)S(1)} %get-tuple-element.337, pred[4,16384]{1,0:T(4,128)(4,1)S(1)} %iota_compare_fusion, ...), kind=kOutput, calls=%fused_computation.46 | convolution fusion | flops 4379246592 | bytes 72163328 | tf_op jit(solution)/shard_map/rhqk,khd->rhqd/dot_general | solution.py:214
  212.8 4.8 %convolution_convert_fusion = bf16[256,4096]{1,0:T(8,128)(2,1)} fusion(bf16[256,512]{1,0:T(8,128)(2,1)S(1)} %reshape_transpose_reshape.4, bf16[512,4096]{1,0:T(8,128)(2,1)} %param.25), kind=kOutput, calls=%fused_computation.36 | convolution fusion | flops 1074790400 | bytes 6553600 | tf_op jit(solution)/shard_map/dot_general | solution.py:224
  219.8 33.7 %reduce-scatter.2.cloned.1.call-done = bf16[32,4096]{1,0:T(8,128)(2,1)} async-done(((bf16[256,4096]{1,0:T(8,128)(2,1)}), bf16[32,4096]{1,0:T(8,128)(2,1)}) %reduce-scatter.2.cloned.1.call-update) | async-done | bytes 262160 | tf_op jit(solution)/shard_map/reduce_scatter | solution.py:223
  (165 shorter events, 39.4 us)
Async XLA Ops:
  7.2 84.3 %copy-start = (bf16[4096,128]{1,0:T(8,128)(2,1)S(1)}, bf16[4096,128]{1,0:T(8,128)(2,1)}, u32[]{:S(2)}) copy-start(bf16[4096,128]{1,0:T(8,128)(2,1)} %param.23) | copy-start | bytes 3145732
  7.2 34.1 %all-gather.3.cloned.1.call-start = ((), (), s32[]{:S(2)}) async-start(), calls=%async_computation.2 | async-start | bytes 2359296 | tf_op jit(solution)/shard_map/all_gather | solution.py:147
  14.0 12.6 %copy-start.14 = (s32[4]{0:T(128)S(1)}, s32[4]{0:T(128)}, u32[]{:S(2)}) copy-start(s32[4]{0:T(128)} %param.31) | copy-start | bytes 52
  14.0 12.8 %copy-start.15 = (s32[128]{0:T(128)S(1)}, s32[128]{0:T(128)}, u32[]{:S(2)}) copy-start(s32[128]{0:T(128)} %param.30) | copy-start | bytes 1540
  14.0 13.1 %copy-start.16 = (s32[4,64]{1,0:T(4,128)S(1)}, s32[4,64]{1,0:T(4,128)}, u32[]{:S(2)}) copy-start(s32[4,64]{1,0:T(4,128)} %param.32) | copy-start | bytes 3076
  14.1 119.9 %all-to-all-start = ((bf16[32,512,128]{2,1,0:T(8,128)(2,1)}), bf16[32,512,128]{2,1,0:T(8,128)(2,1)}, u32[]{:S(2)}, u32[]{:S(2)}) async-start(bf16[32,512,128]{2,1,0:T(8,128)(2,1)} %stack.2), calls=%async_computation | async-start | bytes 8388608 | tf_op jit(solution)/shard_map/all_to_all | solution.py:10
  25.8 160.7 %all-gather.5.cloned.1.call-start = ((), (), s32[]{:S(2)}) async-start(), calls=%async_computation.3 | async-start | bytes 4325376 | tf_op jit(solution)/shard_map/all_gather | solution.py:200
  26.6 226.9 %reduce-scatter.2.cloned.1.call-start = ((), (), s32[]{:S(2)}) async-start(), calls=%async_computation.4 | async-start | bytes 2359296 | tf_op jit(solution)/shard_map/reduce_scatter | solution.py:223
  46.0 0.9 copy-start.2
  46.0 0.9 copy-start.4
  46.9 44.5 %copy-start.1 = (bf16[256,4096]{1,0:T(8,128)(2,1)S(1)}, bf16[256,4096]{1,0:T(8,128)(2,1)}, u32[]{:S(2)}) copy-start(bf16[256,4096]{1,0:T(8,128)(2,1)} %all-gather.3.cloned.1.call-done) | copy-start | bytes 6291460
  91.4 7.7 %copy-start.11 = (f32[4,1,256]{2,1,0:T(1,128)}, f32[4,1,256]{2,1,0:T(1,128)S(1)}, u32[]{:S(2)}) copy-start(f32[4,1,256]{2,1,0:T(1,128)S(1)} %get-tuple-element.269) | copy-start | bytes 12292
  91.4 42.5 %copy-start.3 = (bf16[256,4,64]{2,1,0:T(4,128)(2,1)S(1)}, bf16[256,4,64]{2,1,0:T(4,128)(2,1)}, u32[]{:S(2)}) copy-start(bf16[256,4,64]{2,1,0:T(4,128)(2,1)} %copy-done.2) | copy-start | bytes 393220
  97.1 0.6 copy-start.7
  99.1 0.7 copy-start.5
  161.0 24.4 %copy-start.12 = (f32[4,1,256]{2,1,0:T(1,128)S(1)}, f32[4,1,256]{2,1,0:T(1,128)}, u32[]{:S(2)}) copy-start(f32[4,1,256]{2,1,0:T(1,128)} %copy-done.11) | copy-start | bytes 12292
  161.0 24.5 %copy-start.6 = (f32[4,256,64]{1,2,0:T(8,128)S(1)}, f32[4,256,64]{1,2,0:T(8,128)}, u32[]{:S(2)}) copy-start(f32[4,256,64]{1,2,0:T(8,128)} %copy-done.5) | copy-start | bytes 786436
  161.0 24.4 %copy-start.9 = (bf16[256,128]{1,0:T(8,128)(2,1)S(1)}, bf16[256,128]{1,0:T(8,128)(2,1)}, u32[]{:S(2)}) copy-start(bf16[256,128]{1,0:T(8,128)(2,1)} %convolution_convert_fusion.1) | copy-start | bytes 196612
  161.0 24.4 %copy-start.10 = (f32[4,1,256,128]{3,2,1,0:T(8,128)S(1)}, f32[4,1,256,128]{3,2,1,0:T(8,128)}, u32[]{:S(2)}) copy-start(f32[4,1,256,128]{3,2,1,0:T(8,128)} %get-tuple-element.268) | copy-start | bytes 1572868
  212.8 4.9 %copy-start.13 = (s32[4,8]{1,0:T(4,128)S(1)}, s32[4,8]{1,0:T(4,128)}, u32[]{:S(2)}) copy-start(s32[4,8]{1,0:T(4,128)} %param.33) | copy-start | bytes 388
  212.8 5.7 %copy-start.8 = (bf16[4,64,128]{2,1,0:T(8,128)(2,1)S(1)}, bf16[4,64,128]{2,1,0:T(8,128)(2,1)}, u32[]{:S(2)}) copy-start(bf16[4,64,128]{2,1,0:T(8,128)(2,1)} %copy-done.7) | copy-start | bytes 196612
Sparse Core Ops, SparseCore 0:
  10.4 30.7 all-gather.2
  43.8 103.3 all-gather.4
  217.8 35.6 reduce-scatter.1
